TPU v7x, 256 devices: a whole 4x4x8 slice. The times are simulated.
256 devices in a mesh: dp: 32 (over x, z), comp: 8 (over y, core).
Axes of the slice: x: 4, y: 4, z: 8, core: 2. Of those that a mesh axis runs over, the one named last changes fastest.
Arguments:
- embeddings: float32 [32768, 1024], P('dp'), may hold values from -6 to 6
- means: float32 [8192, 1024], P(('comp', 'dp')), may hold values from -2 to 2
- variances: float32 [8192, 1024], P(('comp', 'dp')), may hold values from 0.7 to 1.4
- log_weights: float32 [8192], P(('comp', 'dp')), may hold values from -2 to 0
Outputs:
- new_means: float32 [8192, 1024], P(('comp', 'dp'))
- new_variances: float32 [8192, 1024], P(('comp', 'dp'))
- new_weights: float32 [8192], P(('comp', 'dp'))
- row_loglik: float32 [32768], P('dp')
All inputs are finite; a program needn't handle non-finite values.
Results may differ from a plain program's by a relative error of at most 0.00045.
Values sent between devices are 32-bit elements; how exact they have to be, the bound alone decides.
A program may use at most 128 MiB of HBM per device.

v0:
```python
import jax
import jax.numpy as jnp
from jax import lax
from jax.sharding import PartitionSpec as P

circle_log = 1.8378770664093453


def component_terms(means, variances, log_weights):
    precision = 1.0 / variances
    scaled = means * precision
    width = means.shape[1]
    offset = (
        log_weights
        - 0.5 * jnp.sum(jnp.log(variances), axis=1)
        - 0.5 * jnp.sum(means * scaled, axis=1)
        - 0.5 * width * circle_log
    )
    return (precision, scaled, offset)


def row_scores(block, squares, precision, scaled, offset):
    highest = lax.Precision.HIGHEST
    quad = jnp.dot(squares, precision.T, precision=highest, preferred_element_type=jnp.float32)
    cross = jnp.dot(block, scaled.T, precision=highest, preferred_element_type=jnp.float32)
    return offset[None, :] + cross - 0.5 * quad


def weighted_sum(resp, values):
    return lax.dot_general(
        resp,
        values,
        (((0,), (0,)), ((), ())),
        precision=lax.Precision.HIGHEST,
        preferred_element_type=jnp.float32,
    )


def per_device(embeddings, means, variances, log_weights):
    squares = embeddings * embeddings
    precision, scaled, offset = component_terms(
        lax.all_gather(means, "dp", axis=0, tiled=True),
        lax.all_gather(variances, "dp", axis=0, tiled=True),
        lax.all_gather(log_weights, "dp", axis=0, tiled=True),
    )
    scores = row_scores(embeddings, squares, precision, scaled, offset)
    local_peak = jnp.max(scores, axis=1)
    peak = lax.pmax(local_peak, "comp")
    total = lax.psum(jnp.sum(jnp.exp(scores - peak[:, None]), axis=1), "comp")
    row_loglik = peak + jnp.log(total)
    resp = jnp.exp(scores - row_loglik[:, None])
    summed = lax.psum_scatter(
        jnp.concatenate([weighted_sum(resp, embeddings), weighted_sum(resp, squares)], axis=1),
        "dp",
        scatter_dimension=0,
        tiled=True,
    )
    counts = lax.psum_scatter(jnp.sum(resp, axis=0), "dp", scatter_dimension=0, tiled=True)
    width = embeddings.shape[1]
    first = summed[:, :width]
    second = summed[:, width:]
    denom = (counts + 1.0)[:, None]
    new_means = (first + means) / denom
    new_variances = (second + variances + means * means) / denom - new_means * new_means
    new_weights = counts / (embeddings.shape[0] * lax.axis_size("dp"))
    return (new_means, new_variances, new_weights, row_loglik)


def solution(mesh):
    return jax.shard_map(
        per_device,
        mesh=mesh,
        in_specs=(
            P("dp", None),
            P(("comp", "dp"), None),
            P(("comp", "dp"), None),
            P(("comp", "dp")),
        ),
        out_specs=(P(("comp", "dp"), None), P(("comp", "dp"), None), P(("comp", "dp")), P("dp")),
        check_vma=False,
    )
```

profile of v0, /device:TPU:8, one launch (start us, length us, event | category | flops | bytes accessed | tf_op | source)
XLA Modules:
  0.0 516.7 jit_solution(10036778705342761832)
XLA Ops:
  7.2 0.7 all-gather.5.cloned.1.call-update
  7.9 0.7 all-gather.3.cloned.1.call-update
  8.6 0.0 reduce-scatter.4.cloned.1.call-start
  8.7 1.3 fusion.17
  10.7 0.9 dynamic-update-slice
  11.6 78.0 %all-reduce = f32[1024]{0:T(1024)S(1)} all-reduce(f32[1024]{0:T(1024)S(1)} %dynamic-update-slice), channel_id=1, replica_groups=mesh['dp'=32,'comp'=8] {'dp'}, use_global_device_ids=true, to_apply=%add | all-reduce | flops 1024 | bytes 8192
  89.6 5.7 %all-gather.5.cloned.1.call-done = f32[1024,1024]{1,0:T(8,128)} async-done(((f32[32,1024]{1,0:T(8,128)}), f32[1024,1024]{1,0:T(8,128)}) %all-gather.5.cloned.1.call-update) | async-done | bytes 4194320 | tf_op jit(solution)/shard_map/all_gather | solution.py:42
  95.3 81.7 %all-gather.3.cloned.1.call-done = f32[1024,1024]{1,0:T(8,128)} async-done(((f32[32,1024]{1,0:T(8,128)}), f32[1024,1024]{1,0:T(8,128)}) %all-gather.3.cloned.1.call-update) | async-done | bytes 4194320 | tf_op jit(solution)/shard_map/all_gather | solution.py:43
  177.0 5.1 log_reduce_fusion
  182.1 0.7 copy-done.6
  182.9 13.6 %fusion.2 = f32[1024,1024]{0,1:T(8,128)S(1)} fusion(f32[1024,1024]{1,0:T(8,128)S(1)} %copy-done.6, f32[1024,1024]{1,0:T(8,128)S(1)} %copy-done.2), kind=kOutput, calls=%fused_computation.8 | convolution fusion | flops 12886999040 | bytes 12582912 | tf_op jit(solution)/shard_map/dot_general | solution.py:24
  196.4 15.2 %fusion.18 = (f32[1024]{0:T(1024)S(1)}, f32[1024,1024]{0,1:T(8,128)}) fusion(f32[1024,1024]{0,1:T(8,128)S(1)} %fusion.2, f32[1024,1024]{1,0:T(8,128)S(1)} %copy-done.6, f32[1024,1024]{1,0:T(8,128)S(1)} %copy-done.1, f32[1024,1024]{1,0:T(8,128)S(1)} %copy-done.2, f32[1024]{0:T(1024)S(1)} %subtract_add_fusion), kind=kOutput, calls=%fused_computation.28 | convolution fusion | flops 12891192320 | bytes 20979712 | tf_op jit(solution)/shard_map/dot_general | solution.py:25
  211.7 10.0 %pmax.7 = f32[1024]{0:T(1024)S(1)} all-reduce(f32[1024]{0:T(1024)S(1)} %get-tuple-element.20), channel_id=1, replica_groups=mesh['dp'=32,'comp'=8] {'comp'}, use_global_device_ids=true, to_apply=%region_3.0 | all-reduce | flops 1024 | bytes 8192 | tf_op jit(solution)/shard_map/pmax | solution.py:48
  221.6 2.8 exponential_reduce_fusion
  224.4 12.4 %psum.7 = f32[1024]{0:T(1024)S(1)} all-reduce(f32[1024]{0:T(1024)S(1)} %exponential_reduce_fusion), channel_id=1, replica_groups=mesh['dp'=32,'comp'=8] {'comp'}, use_global_device_ids=true, to_apply=%region_5.0 | all-reduce | flops 1024 | bytes 8192 | tf_op jit(solution)/shard_map/psum | solution.py:49
  236.9 17.7 %fusion = f32[1024,1024]{0,1:T(8,128)S(1)} fusion(f32[1024,1024]{1,0:T(8,128)} %param.4, f32[1024,1024]{0,1:T(8,128)} %get-tuple-element.21, f32[1024]{0:T(1024)S(1)} %log_add_fusion), kind=kOutput, calls=%fused_computation.6 | convolution fusion | flops 12886999040 | bytes 12587008 | tf_op jit(solution)/shard_map/dot_general | solution.py:30
  254.6 13.8 %fusion.7 = f32[1024,1024]{0,1:T(8,128)S(1)} fusion(f32[1024,1024]{1,0:T(8,128)S(1)} %copy-done.7, f32[1024,1024]{0,1:T(8,128)S(1)} %copy-done, f32[1024]{0:T(1024)S(1)} %log_add_fusion), kind=kOutput, calls=%fused_computation.13 | convolution fusion | flops 12885950464 | bytes 12587008 | tf_op jit(solution)/shard_map/dot_general | solution.py:30
  268.5 4.1 pad_maximum_fusion
  272.5 9.1 %copy.22 = f32[1024,2048]{1,0:T(8,128)} copy(f32[1024,2048]{0,1:T(8,128)} %pad_maximum_fusion) | data formatting | bytes 16777216
  282.4 2.8 fusion.6
  285.2 72.8 %all-reduce.1 = f32[1024]{0:T(1024)S(1)} all-reduce(f32[1024]{0:T(1024)S(1)} %fusion.6), channel_id=3, replica_groups=mesh['dp'=32,'comp'=8] {'dp'}, use_global_device_ids=true, to_apply=%region_8.0.clone | all-reduce | flops 1024 | bytes 8192
  358.0 0.6 broadcast_multiply_fusion
  358.6 149.4 %reduce-scatter.4.cloned.1.call-done = f32[32,2048]{1,0:T(8,128)} async-done(((f32[1024,2048]{1,0:T(8,128)}), f32[32,2048]{1,0:T(8,128)}) %reduce-scatter.4.cloned.1.call-update) | async-done | bytes 262160 | tf_op jit(solution)/shard_map/reduce_scatter | solution.py:52
  507.9 1.8 fusion.14
  (21 shorter events, 0.1 us)
Async XLA Ops:
  7.2 88.1 %all-gather.5.cloned.1.call-start = ((), (), s32[]{:S(2)}) async-start(), calls=%async_computation.2 | async-start | bytes 4325376 | tf_op jit(solution)/shard_map/all_gather | solution.py:42
  7.9 169.1 %all-gather.3.cloned.1.call-start = ((), (), s32[]{:S(2)}) async-start(), calls=%async_computation.1 | async-start | bytes 4325376 | tf_op jit(solution)/shard_map/all_gather | solution.py:43
  8.6 499.3 %reduce-scatter.4.cloned.1.call-start = ((), (), s32[]{:S(2)}) async-start(), calls=%async_computation.3 | async-start | bytes 8650752 | tf_op jit(solution)/shard_map/reduce_scatter | solution.py:52
  177.0 5.2 copy-start.2
  177.0 5.9 %copy-start.6 = (f32[1024,1024]{1,0:T(8,128)S(1)}, f32[1024,1024]{1,0:T(8,128)}, u32[]{:S(2)}) copy-start(f32[1024,1024]{1,0:T(8,128)} %param.4) | copy-start | bytes 12582916
  182.9 13.6 %copy-start.1 = (f32[1024,1024]{1,0:T(8,128)S(1)}, f32[1024,1024]{1,0:T(8,128)}, u32[]{:S(2)}) copy-start(f32[1024,1024]{1,0:T(8,128)} %all-gather.5.cloned.1.call-done) | copy-start | bytes 12582916
  236.9 45.5 %copy-start.5 = (f32[1024]{0:T(1024)}, f32[1024]{0:T(1024)S(1)}, u32[]{:S(2)}) copy-start(f32[1024]{0:T(1024)S(1)} %log_add_fusion) | copy-start | bytes 12292
  236.9 17.7 %copy-start = (f32[1024,1024]{0,1:T(8,128)S(1)}, f32[1024,1024]{0,1:T(8,128)}, u32[]{:S(2)}) copy-start(f32[1024,1024]{0,1:T(8,128)} %get-tuple-element.21) | copy-start | bytes 12582916
  236.9 17.7 %copy-start.7 = (f32[1024,1024]{1,0:T(8,128)S(1)}, f32[1024,1024]{1,0:T(8,128)}, u32[]{:S(2)}) copy-start(f32[1024,1024]{1,0:T(8,128)} %param.4) | copy-start | bytes 12582916
  281.7 226.3 %copy-start.3 = (f32[32,1024]{1,0:T(8,128)S(1)}, f32[32,1024]{1,0:T(8,128)}, u32[]{:S(2)}) copy-start(f32[32,1024]{1,0:T(8,128)} %param.6) | copy-start | bytes 393220
  281.7 226.2 %copy-start.4 = (f32[32,1024]{1,0:T(8,128)S(1)}, f32[32,1024]{1,0:T(8,128)}, u32[]{:S(2)}) copy-start(f32[32,1024]{1,0:T(8,128)} %param.5) | copy-start | bytes 393220
Sparse Core Ops, SparseCore 0:
  10.6 84.6 all-gather.4
  97.9 79.0 all-gather.2
  281.8 226.0 reduce-scatter.3
where the time goes:
time: 526 us; the launch traced here: 517 us
  waiting for transfers between devices  238 us (45%)
  blocking collectives  173 us (33%)
  matrix products  60.3 us (11%)
  other arithmetic  17.2 us (3%)
  between operations  15.7 us (3%)
  local copies, waits for them, and re-layouts  12.1 us (2%)
    unnamed x2, blocking collectives  151 us
    reduce_scatter x1, waiting for transfers between devices, per_device(): lax.psum_scatter(jnp.concatenate([weighted_sum(resp, embeddings), weighte...  149 us
    all_gather x1, waiting for transfers between devices, per_device(): lax.all_gather(variances, 'dp', axis=0, tiled=True)  81.7 us
    dot_general x2, matrix products, weighted_sum(): lax.dot_general(resp, values, (((0,), (0,)), ((), ())), precision=lax.Pre...  31.5 us
    dot_general x1, matrix products, row_scores(): jnp.dot(block, scaled.T, precision=highest, preferred_element_type=jnp.fl...  15.2 us
    dot_general x1, matrix products, row_scores(): jnp.dot(squares, precision.T, precision=highest, preferred_element_type=j...  13.6 us
    psum x1, blocking collectives, per_device(): total = lax.psum(jnp.sum(jnp.exp(scores - peak[:, None]), axis=1), 'comp')  12.4 us
    unnamed x20, local copies, waits for them, and re-layouts  12.1 us
  transfers between devices with their start and end apart: 3, of which 3 were waited for; matrix products, arithmetic and copies ran while one was open for 1% of the time, Pallas kernels for 0%

commit v1 on v0

--- a/solution.py
+++ b/solution.py
@@ -1,9 +1,20 @@
+import functools
 import jax
 import jax.numpy as jnp
 from jax import lax
 from jax.sharding import PartitionSpec as P
 
 circle_log = 1.8378770664093453
+
+
+def reach_cubes(vector, axis_id):
+    outcome_arr = tuple((vector for _ in range(lax.psum(1, axis_name=axis_id))))
+    z1 = jnp.stack(outcome_arr)
+    later = jnp.concatenate(lax.all_to_all(z1, axis_id, concat_axis=0, split_axis=0), axis=0)
+    return later
+
+
+pair_turns = functools.partial(reach_cubes, axis_id="dp")
 
 
 def component_terms(means, variances, log_weights):
@@ -40,7 +51,7 @@
     squares = embeddings * embeddings
     precision, scaled, offset = component_terms(
         lax.all_gather(means, "dp", axis=0, tiled=True),
-        lax.all_gather(variances, "dp", axis=0, tiled=True),
+        pair_turns(variances),
         lax.all_gather(log_weights, "dp", axis=0, tiled=True),
     )
     scores = row_scores(embeddings, squares, precision, scaled, offset)

time: 526 us -> 550 us (1.046)
  blocking collectives: 173 us -> 263 us
  waiting for transfers between devices: 238 us -> 148 us
  starting transfers between devices: 0.11 us -> 11.7 us
  matrix products: 60.3 us -> 67.1 us
    unnamed x2, blocking collectives: 151 us -> 240 us
    all_gather x1 -> x0, waiting for transfers between devices: 81.7 us -> none  [per_device(): lax.all_gather(variances, 'dp', axis=0, tiled=True)]
    all_to_all x0 -> x1, starting transfers between devices: none -> 11.6 us  [reach_cubes(): lax.all_to_all(z1, axis_id, concat_axis=0, split_axis=0)]
    all_gather x1, waiting for transfers between devices: 5.66 us -> 0.01 us  [per_device(): lax.all_gather(means, 'dp', axis=0, tiled=True)]
    unnamed x20 -> x22, local copies, waits for them, and re-layouts: 12.1 us -> 11.8 us
  transfers between devices with their start and end apart: 3 -> 3, of which waited for: 3 -> 1; matrix products, arithmetic and copies ran while one was open for 1% -> 5% of each run, Pallas kernels for 0% -> 0%
where the time goes in v1:
time: 550 us; the launch traced here: 542 us
  blocking collectives  263 us (48%)
  waiting for transfers between devices  148 us (27%)
  matrix products  67.1 us (12%)
  other arithmetic  21.4 us (4%)
  between operations  15.8 us (3%)
  local copies, waits for them, and re-layouts  15.3 us (3%)
  starting transfers between devices  11.7 us (2%)
    unnamed x2, blocking collectives  240 us
    reduce_scatter x1, waiting for transfers between devices, per_device(): lax.psum_scatter(jnp.concatenate([weighted_sum(resp, embeddings), weighte...  148 us
    dot_general x2, matrix products, weighted_sum(): lax.dot_general(resp, values, (((0,), (0,)), ((), ())), precision=lax.Pre...  31.6 us
    dot_general x1, matrix products, row_scores(): jnp.dot(block, scaled.T, precision=highest, preferred_element_type=jnp.fl...  17.8 us
    dot_general x1, matrix products, row_scores(): jnp.dot(squares, precision.T, precision=highest, preferred_element_type=j...  17.7 us
    psum x1, blocking collectives, per_device(): total = lax.psum(jnp.sum(jnp.exp(scores - peak[:, None]), axis=1), 'comp')  12.4 us
    unnamed x22, local copies, waits for them, and re-layouts  11.8 us
    all_to_all x1, starting transfers between devices, reach_cubes(): lax.all_to_all(z1, axis_id, concat_axis=0, split_axis=0)  11.6 us
  transfers between devices with their start and end apart: 3, of which 1 were waited for; matrix products, arithmetic and copies ran while one was open for 5% of the time, Pallas kernels for 0%

profile of v1, /device:TPU:8, one launch (start us, length us, event | category | flops | bytes accessed | tf_op | source)
XLA Modules:
  0.0 542.3 jit_solution(5614488161369537016)
XLA Ops:
  7.2 3.4 stack.2
  10.6 11.6 %all-to-all-start = ((f32[32,32,1024]{2,1,0:T(8,128)}), f32[32,32,1024]{2,1,0:T(8,128)}, u32[]{:S(2)}, u32[]{:S(2)}) async-start(f32[32,32,1024]{2,1,0:T(8,128)} %stack.2), calls=%async_computation | async-start | bytes 8388608 | tf_op jit(solution)/shard_map/all_to_all | solution.py:13
  22.2 0.7 all-gather.2.cloned.1.call-update
  23.0 0.6 fusion.17
  24.2 0.2 dynamic-update-slice
  24.5 170.2 %all-reduce = f32[1024]{0:T(1024)S(1)} all-reduce(f32[1024]{0:T(1024)S(1)} %dynamic-update-slice), channel_id=1, replica_groups=mesh['dp'=32,'comp'=8] {'dp'}, use_global_device_ids=true, to_apply=%add | all-reduce | flops 1024 | bytes 8192
  194.7 5.2 log_reduce_fusion
  200.0 17.7 %fusion.2 = f32[1024,1024]{0,1:T(8,128)} fusion(f32[1024,1024]{1,0:T(8,128)} %bitcast.10, f32[1024,1024]{1,0:T(8,128)} %param.4), kind=kOutput, calls=%fused_computation.8 | convolution fusion | flops 12885950464 | bytes 12582912 | tf_op jit(solution)/shard_map/dot_general | solution.py:35
  217.7 4.1 multiply_reduce_fusion
  221.8 0.5 copy-done.1
  222.4 1.3 copy-done.2
  223.7 17.8 %fusion.18 = (f32[1024]{0:T(1024)S(1)}, f32[1024,1024]{0,1:T(8,128)}) fusion(f32[1024,1024]{0,1:T(8,128)} %fusion.2, f32[1024,1024]{1,0:T(8,128)} %param.4, f32[1024,1024]{1,0:T(8,128)S(1)} %copy-done.2, f32[1024,1024]{1,0:T(8,128)S(1)} %bitcast.11, f32[1024]{0:T(1024)S(1)} %subtract_add_fusion), kind=kOutput, calls=%fused_computation.29 | convolution fusion | flops 12890143744 | bytes 20979712 | tf_op jit(solution)/shard_map/dot_general | solution.py:36
  241.4 10.0 %pmax.7 = f32[1024]{0:T(1024)S(1)} all-reduce(f32[1024]{0:T(1024)S(1)} %get-tuple-element.20), channel_id=1, replica_groups=mesh['dp'=32,'comp'=8] {'comp'}, use_global_device_ids=true, to_apply=%region_3.0 | all-reduce | flops 1024 | bytes 8192 | tf_op jit(solution)/shard_map/pmax | solution.py:59
  251.4 2.8 exponential_reduce_fusion
  254.2 12.4 %psum.7 = f32[1024]{0:T(1024)S(1)} all-reduce(f32[1024]{0:T(1024)S(1)} %exponential_reduce_fusion), channel_id=1, replica_groups=mesh['dp'=32,'comp'=8] {'comp'}, use_global_device_ids=true, to_apply=%region_5.0 | all-reduce | flops 1024 | bytes 8192 | tf_op jit(solution)/shard_map/psum | solution.py:60
  266.6 17.8 %fusion = f32[1024,1024]{0,1:T(8,128)S(1)} fusion(f32[1024,1024]{1,0:T(8,128)} %param.4, f32[1024,1024]{0,1:T(8,128)} %get-tuple-element.21, f32[1024]{0:T(1024)S(1)} %log_add_fusion), kind=kOutput, calls=%fused_computation.6 | convolution fusion | flops 12886999040 | bytes 12587008 | tf_op jit(solution)/shard_map/dot_general | solution.py:41
  284.5 13.8 %fusion.7 = f32[1024,1024]{0,1:T(8,128)S(1)} fusion(f32[1024,1024]{1,0:T(8,128)S(1)} %copy-done.3, f32[1024,1024]{0,1:T(8,128)S(1)} %copy-done, f32[1024]{0:T(1024)S(1)} %log_add_fusion), kind=kOutput, calls=%fused_computation.13 | convolution fusion | flops 12885950464 | bytes 12587008 | tf_op jit(solution)/shard_map/dot_general | solution.py:41
  298.3 4.1 pad_maximum_fusion
  302.4 9.1 %copy.22 = f32[1024,2048]{1,0:T(8,128)} copy(f32[1024,2048]{0,1:T(8,128)} %pad_maximum_fusion) | data formatting | bytes 16777216
  312.3 2.8 fusion.6
  315.1 70.1 %all-reduce.1 = f32[1024]{0:T(1024)S(1)} all-reduce(f32[1024]{0:T(1024)S(1)} %fusion.6), channel_id=3, replica_groups=mesh['dp'=32,'comp'=8] {'dp'}, use_global_device_ids=true, to_apply=%region_8.0.clone | all-reduce | flops 1024 | bytes 8192
  385.1 0.6 broadcast_multiply_fusion.1
  385.7 147.7 %reduce-scatter.4.cloned.1.call-done = f32[32,2048]{1,0:T(8,128)} async-done(((f32[1024,2048]{1,0:T(8,128)}), f32[32,2048]{1,0:T(8,128)}) %reduce-scatter.4.cloned.1.call-update) | async-done | bytes 262160 | tf_op jit(solution)/shard_map/reduce_scatter | solution.py:63
  533.4 1.8 fusion.14
  (26 shorter events, 0.2 us)
Async XLA Ops:
  10.6 12.4 %copy-start.7 = (u32[256]{0:T(256)S(1)}, u32[256]{0:T(256)}, u32[]{:S(2)}) copy-start(u32[256]{0:T(256)} %constant.21) | copy-start | bytes 3076
  10.6 13.6 %copy-start.8 = (f32[32]{0:T(128)S(1)}, f32[32]{0:T(128)}, u32[]{:S(2)}) copy-start(f32[32]{0:T(128)} %param.7) | copy-start | bytes 388
  10.6 184.1 %all-to-all-start = ((f32[32,32,1024]{2,1,0:T(8,128)}), f32[32,32,1024]{2,1,0:T(8,128)}, u32[]{:S(2)}, u32[]{:S(2)}) async-start(f32[32,32,1024]{2,1,0:T(8,128)} %stack.2), calls=%async_computation | async-start | bytes 8388608 | tf_op jit(solution)/shard_map/all_to_all | solution.py:13
  22.2 195.6 %all-gather.2.cloned.1.call-start = ((), (), s32[]{:S(2)}) async-start(), calls=%async_computation.2 | async-start | bytes 4325376 | tf_op jit(solution)/shard_map/all_gather | solution.py:53
  22.9 510.5 %reduce-scatter.4.cloned.1.call-start = ((), (), s32[]{:S(2)}) async-start(), calls=%async_computation.3 | async-start | bytes 8650752 | tf_op jit(solution)/shard_map/reduce_scatter | solution.py:63
  217.7 4.6 copy-start.1
  217.7 5.9 %copy-start.2 = (f32[1024,1024]{1,0:T(8,128)S(1)}, f32[1024,1024]{1,0:T(8,128)}, u32[]{:S(2)}) copy-start(f32[1024,1024]{1,0:T(8,128)} %all-gather.2.cloned.1.call-done) | copy-start | bytes 12582916
  266.6 45.6 %copy-start.6 = (f32[1024]{0:T(1024)}, f32[1024]{0:T(1024)S(1)}, u32[]{:S(2)}) copy-start(f32[1024]{0:T(1024)S(1)} %log_add_fusion) | copy-start | bytes 12292
  266.6 17.8 %copy-start = (f32[1024,1024]{0,1:T(8,128)S(1)}, f32[1024,1024]{0,1:T(8,128)}, u32[]{:S(2)}) copy-start(f32[1024,1024]{0,1:T(8,128)} %get-tuple-element.21) | copy-start | bytes 12582916
  266.6 17.8 %copy-start.3 = (f32[1024,1024]{1,0:T(8,128)S(1)}, f32[1024,1024]{1,0:T(8,128)}, u32[]{:S(2)}) copy-start(f32[1024,1024]{1,0:T(8,128)} %param.4) | copy-start | bytes 12582916
  311.5 221.9 %copy-start.4 = (f32[32,1024]{1,0:T(8,128)S(1)}, f32[32,1024]{1,0:T(8,128)}, u32[]{:S(2)}) copy-start(f32[32,1024]{1,0:T(8,128)} %param.6) | copy-start | bytes 393220
  311.6 221.8 %copy-start.5 = (f32[32,1024]{1,0:T(8,128)S(1)}, f32[32,1024]{1,0:T(8,128)}, u32[]{:S(2)}) copy-start(f32[32,1024]{1,0:T(8,128)} %param.5) | copy-start | bytes 393220
Sparse Core Ops, SparseCore 0:
  25.6 118.4 all-gather.1
  311.7 221.6 reduce-scatter.3
